TPU v7x, 512 devices: a whole 4x8x8 slice. The times are simulated.
512 devices in a mesh: dp: 16 (over z, core), seq: 32 (over x, y).
Axes of the slice: x: 4, y: 8, z: 8, core: 2. Of those that a mesh axis runs over, the one named last changes fastest.
Arguments:
- inputs: bfloat16 [16, 4096, 4096], P('dp', 'seq'), may hold values from -6 to 6
- out_grads: bfloat16 [16, 4096, 14336], P('dp', 'seq'), may hold values from -6 to 6
- valid: int32 [16, 4096], P('dp', 'seq'), may hold values 0 or 1
- doc_blocks: int32 [16, 4], P('dp'), may hold values from 1 to 16, 32 in all within a row
- doc_ids: int32 [64], replicated, may hold values from 0 to 63, each once
- proj_in: bfloat16 [4096, 64], P('seq'), may hold values from -0.09375 to 0.09375
- proj_out: bfloat16 [14336, 64], P('seq'), may hold values from -0.046875 to 0.046875
- test_grads: bfloat16 [1024, 4096], P('seq'), may hold values from -192 to 192
Outputs:
- scores: float32 [64, 1024], P(None, 'seq')
Inputs may be any that keep to these rules, and one draw needn't show every extreme that they name: `doc_blocks`: each group's lengths sum to 32; the largest is 16 in every group. `doc_ids`: every document number appears once.
All inputs are finite; a program needn't handle non-finite values. No bound on the sum of `valid` on one device may be relied on, other than what follows from the above.
Results may differ from a plain program's by a relative error of at most 0.0003.
Values may be sent and summed in bfloat16 or wider, within the bound.
A program may use at most 64 MiB of HBM per device.

v0:
```python
import jax
import jax.numpy as jnp
from jax import lax
from jax.sharding import PartitionSpec as P

PROJ_OUT = 64
FEAT = 4096
BLOCK = 128
DOC_GRP = 4


def per_device(inputs, out_grads, valid, doc_blocks, doc_ids, proj_in, proj_out, test_grads):
    tokens = inputs[0]
    outgrad = out_grads[0]
    slots = tokens.shape[0]
    columns = tokens
    px = jnp.dot(
        columns,
        lax.all_gather(proj_in, "seq", axis=0, tiled=True),
        preferred_element_type=jnp.float32,
    )
    columns = outgrad
    pg = jnp.dot(
        columns,
        lax.all_gather(proj_out, "seq", axis=0, tiled=True),
        preferred_element_type=jnp.float32,
    )
    ends = jnp.cumsum(doc_blocks[0])
    position = lax.axis_index("seq") * slots + jnp.arange(slots, dtype=jnp.int32)
    blk = position // BLOCK
    owner = jnp.sum((blk[:, None] >= ends[None, :]).astype(jnp.int32), axis=1)
    onehot = (
        (owner[:, None] == jnp.arange(DOC_GRP, dtype=jnp.int32)[None, :]) & (valid[0][:, None] == 1)
    ).astype(jnp.float32)
    weighted = (onehot[:, :, None] * pg[:, None, :]).reshape(slots, DOC_GRP * PROJ_OUT)
    partial_grads = jnp.dot(weighted.T, px, precision=lax.Precision.HIGHEST).reshape(DOC_GRP, FEAT)
    ndocs = DOC_GRP * lax.axis_size("dp")
    group_grads = lax.psum(partial_grads, "seq")
    doc_grads = lax.all_gather(group_grads, "dp", axis=0, tiled=True)
    gram = jnp.dot(doc_grads, doc_grads.T, precision=lax.Precision.HIGHEST)
    cross = jnp.dot(doc_grads, test_grads.astype(jnp.float32).T, precision=lax.Precision.HIGHEST)
    damp = 0.1 * jnp.trace(gram) / ndocs
    matrix = gram / ndocs + damp * jnp.eye(ndocs, dtype=jnp.float32)
    factor = jnp.linalg.cholesky(matrix)
    middle = lax.linalg.triangular_solve(factor, cross, left_side=True, lower=True)
    solved = lax.linalg.triangular_solve(
        factor, middle, left_side=True, lower=True, transpose_a=True
    )
    placing = (doc_ids[None, :] == jnp.arange(ndocs, dtype=jnp.int32)[:, None]).astype(jnp.float32)
    return jnp.dot(placing, solved, precision=lax.Precision.HIGHEST)


def solution(mesh):
    in_specs = (
        P("dp", "seq", None),
        P("dp", "seq", None),
        P("dp", "seq"),
        P("dp", None),
        P(),
        P("seq", None),
        P("seq", None),
        P("seq", None),
    )
    out_specs = P(None, "seq")
    return jax.shard_map(
        per_device, mesh=mesh, in_specs=in_specs, out_specs=out_specs, check_vma=False
    )
```

profile of v0, /device:TPU:1, one launch (start us, length us, event | category | flops | bytes accessed | tf_op | source)
XLA Modules:
  0.0 325.9 jit_solution(14330074124522014039)
XLA Ops:
  6.5 0.7 all-gather.5.cloned.1.call-update
  7.3 0.8 reduce-window.8
  8.1 0.1 convert_reduce_fusion
  8.2 41.4 %all_gather.10 = bf16[4096,64]{0,1:T(8,128)(2,1)S(1)} all-gather(bf16[128,64]{0,1:T(8,128)(2,1)} %param.13), channel_id=1, replica_groups=mesh['dp'=16,'seq'=32] {'seq'}, dimensions={0}, use_global_device_ids=true | all-gather | bytes 540672 | tf_op jit(solution)/shard_map/all_gather | solution.py:19
  49.6 0.7 compare_bitcast_fusion
  50.3 0.5 fusion.2
  50.8 44.7 %all-gather.5.cloned.1.call-done = bf16[32,448,64]{1,2,0:T(8,128)(2,1)} async-done(((bf16[1,448,64]{1,2,0:T(8,128)(2,1)}), bf16[32,448,64]{1,2,0:T(8,128)(2,1)}) %all-gather.5.cloned.1.call-update) | async-done | bytes 1835024 | tf_op jit(solution)/shard_map/all_gather | solution.py:25
  95.6 2.8 copy.20
  98.3 3.4 %reshape.113 = bf16[14336,64]{0,1:T(8,128)(2,1)} reshape(bf16[32,448,64]{1,0,2:T(8,128)(2,1)S(1)} %copy.20) | data formatting | bytes 3670016
  101.7 4.0 %fusion = f32[128,64]{0,1:T(8,128)S(1)} fusion(bf16[14336,64]{0,1:T(8,128)(2,1)} %reshape.113, bf16[1,128,14336]{2,1,0:T(8,128)(2,1)} %param.9), kind=kOutput, calls=%fused_computation | convolution fusion | flops 234881024 | bytes 5537792 | tf_op jit(solution)/shard_map/dot_general | solution.py:23
  105.7 0.3 fusion.15
  106.0 0.7 reshape.111
  106.8 147.6 %all-reduce.2.cloned.1.call-done = f32[4,4096]{1,0:T(4,128)} async-done(((f32[4,4096]{1,0:T(4,128)}), f32[4,4096]{1,0:T(4,128)}) %all-reduce.2.cloned.1.call-update) | async-done | bytes 65552 | tf_op jit(solution)/shard_map/psum | solution.py:38
  254.4 47.1 %all-gather.7.cloned.1.call-done = f32[16,4,4096]{2,1,0:T(4,128)} async-done(((f32[1,4,4096]{2,1,0:T(4,128)}), f32[16,4,4096]{2,1,0:T(4,128)}) %all-gather.7.cloned.1.call-update) | async-done | bytes 1048592 | tf_op jit(solution)/shard_map/all_gather | solution.py:39
  301.5 1.6 reshape.115
  303.1 1.6 select_reduce_fusion.1
  305.6 5.8 %cholesky.17 = f32[64,64]{1,0:T(8,128)S(1)} custom-call(f32[64,64]{1,0:T(8,128)S(1)} %fusion.10), custom_call_target="Cholesky" | custom-call | tf_op jit(solution)/shard_map/jit(cholesky)/cholesky | solution.py:44
  311.4 0.6 compare_reduce_fusion
  312.1 0.7 fusion.4
  312.8 4.9 %custom-call.8 = f32[1,64,64]{1,2,0:T(8,128)S(1)} custom-call(f32[1,64,64]{2,1,0:T(8,128)S(1)} %fusion.4), custom_call_target="InvertDiagBlocksLowerTriangular" | custom-call | tf_op jit(solution)/shard_map/triangular_solve | solution.py:46
  317.7 0.6 fusion.16
  318.3 0.1 fusion.7
  318.4 0.2 fusion.5
  318.6 0.8 fusion.11
  (19 shorter events, 0.4 us)
Async XLA Ops:
  6.5 43.8 %copy-start = (bf16[1,128,4096]{2,1,0:T(8,128)(2,1)S(1)}, bf16[1,128,4096]{2,1,0:T(8,128)(2,1)}, u32[]{:S(2)}) copy-start(bf16[1,128,4096]{2,1,0:T(8,128)(2,1)} %param.8) | copy-start | bytes 3145732
  6.5 89.0 %all-gather.5.cloned.1.call-start = ((), (), s32[]{:S(2)}) async-start(), calls=%async_computation.1 | async-start | bytes 2162688 | tf_op jit(solution)/shard_map/all_gather | solution.py:25
  7.3 247.2 %all-reduce.2.cloned.1.call-start = ((), (), s32[]{:S(2)}) async-start(), calls=%async_computation | async-start | bytes 131072 | tf_op jit(solution)/shard_map/psum | solution.py:38
  106.7 194.8 %all-gather.7.cloned.1.call-start = ((), (), s32[]{:S(2)}) async-start(), calls=%async_computation.2 | async-start | bytes 1114112 | tf_op jit(solution)/shard_map/all_gather | solution.py:39
  254.4 63.2 %copy-start.1 = (bf16[32,4096]{1,0:T(8,128)(2,1)S(1)}, bf16[32,4096]{1,0:T(8,128)(2,1)}, u32[]{:S(2)}) copy-start(bf16[32,4096]{1,0:T(8,128)(2,1)} %param.15) | copy-start | bytes 786436
  303.1 15.5 %copy-start.2 = (s32[64]{0:T(128)S(1)}, s32[64]{0:T(128)}, u32[]{:S(2)}) copy-start(s32[64]{0:T(128)} %param.12) | copy-start | bytes 772
Sparse Core Ops, SparseCore 0:
  10.5 84.9 all-gather.4
  106.8 147.5 all-reduce.1
  256.5 44.9 all-gather.6
where the time goes:
time: 326 us
  waiting for transfers between devices  240 us (74%)
  blocking collectives  41.4 us (13%)
  between operations  13.9 us (4%)
  other arithmetic  13.7 us (4%)
  local copies, waits for them, and re-layouts  8.61 us (3%)
  matrix products  8 us (2%)
    psum x1, waiting for transfers between devices, per_device(): group_grads = lax.psum(partial_grads, 'seq')  148 us
    all_gather x1, waiting for transfers between devices, per_device(): doc_grads = lax.all_gather(group_grads, 'dp', axis=0, tiled=True)  47.1 us
    all_gather x1, waiting for transfers between devices, per_device(): lax.all_gather(proj_out, 'seq', axis=0, tiled=True)  44.7 us
    all_gather x1, blocking collectives, per_device(): lax.all_gather(proj_in, 'seq', axis=0, tiled=True)  41.4 us
  transfers between devices with their start and end apart: 3, of which 3 were waited for; matrix products, arithmetic and copies ran while one was open for 1% of the time, Pallas kernels for 0%

commit v1 on v0

--- a/solution.py
+++ b/solution.py
@@ -7,6 +7,16 @@
 FEAT = 4096
 BLOCK = 128
 DOC_GRP = 4
+
+
+def gather_by_hops(x, axis, along):
+    size = lax.axis_size(axis)
+    held, blocks = (x, [x])
+    for _ in range(size - 1):
+        held = lax.ppermute(held, axis, [(i, (i + 1) % size) for i in range(size)])
+        blocks.insert(0, held)
+    line = jnp.concatenate(blocks, axis=along)
+    return jnp.roll(line, (lax.axis_index(axis) + 1) * x.shape[along], axis=along)
 
 
 def per_device(inputs, out_grads, valid, doc_blocks, doc_ids, proj_in, proj_out, test_grads):
@@ -36,7 +46,7 @@
     partial_grads = jnp.dot(weighted.T, px, precision=lax.Precision.HIGHEST).reshape(DOC_GRP, FEAT)
     ndocs = DOC_GRP * lax.axis_size("dp")
     group_grads = lax.psum(partial_grads, "seq")
-    doc_grads = lax.all_gather(group_grads, "dp", axis=0, tiled=True)
+    doc_grads = gather_by_hops(group_grads, "dp", 0)
     gram = jnp.dot(doc_grads, doc_grads.T, precision=lax.Precision.HIGHEST)
     cross = jnp.dot(doc_grads, test_grads.astype(jnp.float32).T, precision=lax.Precision.HIGHEST)
     damp = 0.1 * jnp.trace(gram) / ndocs

time: 326 us -> 372 us (1.14)
  local copies, waits for them, and re-layouts: 8.61 us -> 23.2 us
  waiting for transfers between devices: 240 us -> 254 us
  starting transfers between devices: 0.08 us -> 13 us
    ppermute x0 -> x15, waiting for transfers between devices: none -> 60.9 us  [gather_by_hops(): held = lax.ppermute(held, axis, [(i, (i + 1) % size) for i in range(size)])]
    all_gather x1 -> x0, waiting for transfers between devices: 47.1 us -> none  [per_device(): doc_grads = lax.all_gather(group_grads, 'dp', axis=0, tiled=True)]
    ppermute x0 -> x15, starting transfers between devices: none -> 12.9 us  [gather_by_hops(): held = lax.ppermute(held, axis, [(i, (i + 1) % size) for i in range(size)])]
    concatenate x0 -> x1, local copies, waits for them, and re-layouts: none -> 11.2 us  [gather_by_hops(): jnp.roll(line, (lax.axis_index(axis) + 1) * x.shape[along], axis=along)]
    unnamed x8 -> x21, local copies, waits for them, and re-layouts: 4.99 us -> 8.42 us
  transfers between devices with their start and end apart: 3 -> 17, of which waited for: 3 -> 17; matrix products, arithmetic and copies ran while one was open for 1% -> 1% of each run, Pallas kernels for 0% -> 0%
where the time goes in v1:
time: 372 us; the launch traced here: 369 us
  waiting for transfers between devices  254 us (68%)
  blocking collectives  41.4 us (11%)
  local copies, waits for them, and re-layouts  23.2 us (6%)
  between operations  14.2 us (4%)
  other arithmetic  13.7 us (4%)
  starting transfers between devices  13 us (3%)
  matrix products  9.07 us (2%)
    psum x1, waiting for transfers between devices, per_device(): group_grads = lax.psum(partial_grads, 'seq')  148 us
    ppermute x15, waiting for transfers between devices, gather_by_hops(): held = lax.ppermute(held, axis, [(i, (i + 1) % size) for i in range(size)])  60.9 us
    all_gather x1, waiting for transfers between devices, per_device(): lax.all_gather(proj_out, 'seq', axis=0, tiled=True)  44.7 us
    all_gather x1, blocking collectives, per_device(): lax.all_gather(proj_in, 'seq', axis=0, tiled=True)  41.4 us
    ppermute x15, starting transfers between devices, gather_by_hops(): held = lax.ppermute(held, axis, [(i, (i + 1) % size) for i in range(size)])  12.9 us
    concatenate x1, local copies, waits for them, and re-layouts, gather_by_hops(): jnp.roll(line, (lax.axis_index(axis) + 1) * x.shape[along], axis=along)  11.2 us
    unnamed x21, local copies, waits for them, and re-layouts  8.42 us
  transfers between devices with their start and end apart: 17, of which 17 were waited for; matrix products, arithmetic and copies ran while one was open for 1% of the time, Pallas kernels for 0%

profile of v1, /device:TPU:1, one launch (start us, length us, event | category | flops | bytes accessed | tf_op | source)
XLA Modules:
  0.0 368.6 jit_solution(16707502477458748978)
XLA Ops:
  8.2 41.4 %all_gather.7 = bf16[4096,64]{0,1:T(8,128)(2,1)S(1)} all-gather(bf16[128,64]{0,1:T(8,128)(2,1)} %param.13), channel_id=1, replica_groups=mesh['dp'=16,'seq'=32] {'seq'}, dimensions={0}, use_global_device_ids=true | all-gather | bytes 540672 | tf_op jit(solution)/shard_map/all_gather | solution.py:29
  50.8 44.7 %all-gather.3.cloned.1.call-done = bf16[32,448,64]{1,2,0:T(8,128)(2,1)} async-done(((bf16[1,448,64]{1,2,0:T(8,128)(2,1)}), bf16[32,448,64]{1,2,0:T(8,128)(2,1)}) %all-gather.3.cloned.1.call-update) | async-done | bytes 1835024 | tf_op jit(solution)/shard_map/all_gather | solution.py:35
  95.6 2.8 copy.20
  98.3 3.4 reshape.113
  101.7 4.0 %fusion = f32[128,64]{0,1:T(8,128)S(1)} fusion(bf16[14336,64]{0,1:T(8,128)(2,1)} %reshape.113, bf16[1,128,14336]{2,1,0:T(8,128)(2,1)} %param.9), kind=kOutput, calls=%fused_computation | convolution fusion | flops 234881024 | bytes 5537792 | tf_op jit(solution)/shard_map/dot_general | solution.py:33
  106.8 147.7 %all-reduce.2.cloned.1.call-done = f32[4,4096]{1,0:T(4,128)} async-done(((f32[4,4096]{1,0:T(4,128)}), f32[4,4096]{1,0:T(4,128)}) %all-reduce.2.cloned.1.call-update) | async-done | bytes 65552 | tf_op jit(solution)/shard_map/psum | solution.py:48
  254.5 5.9 %collective-permute-start = (f32[4,4096]{1,0:T(4,128)}, f32[4,4096]{1,0:T(4,128)S(1)}, u32[]{:S(2)}, u32[]{:S(2)}) collective-permute-start(f32[4,4096]{1,0:T(4,128)} %all-reduce.2.cloned.1.call-done), channel_id=1, source_target_pairs={{0,32},{32,64},{64,96},{96,128},{128,160},{160,192},{192,224},{224... | collective-permute-start | bytes 196616 | tf_op jit(solution)/shard_map/ppermute | solution.py:16
  262.1 2.3 collective-permute-start.1
  265.6 2.4 collective-permute-start.2
  271.7 3.1 collective-permute-done.3
  275.4 4.3 %collective-permute-done.4 = f32[4,4096]{1,0:T(4,128)S(1)} collective-permute-done((f32[4,4096]{1,0:T(4,128)S(1)}, f32[4,4096]{1,0:T(4,128)S(1)}, u32[]{:S(2)}, u32[]{:S(2)}) %collective-permute-start.4) | collective-permute-done | bytes 65568 | tf_op jit(solution)/shard_map/ppermute | solution.py:16
  279.7 4.9 %collective-permute-done.5 = f32[4,4096]{1,0:T(4,128)S(1)} collective-permute-done((f32[4,4096]{1,0:T(4,128)S(1)}, f32[4,4096]{1,0:T(4,128)S(1)}, u32[]{:S(2)}, u32[]{:S(2)}) %collective-permute-start.5) | collective-permute-done | bytes 65568 | tf_op jit(solution)/shard_map/ppermute | solution.py:16
  284.6 4.9 %collective-permute-done.6 = f32[4,4096]{1,0:T(4,128)S(1)} collective-permute-done((f32[4,4096]{1,0:T(4,128)S(1)}, f32[4,4096]{1,0:T(4,128)S(1)}, u32[]{:S(2)}, u32[]{:S(2)}) %collective-permute-start.6) | collective-permute-done | bytes 65568 | tf_op jit(solution)/shard_map/ppermute | solution.py:16
  290.2 4.9 %collective-permute-done.7 = f32[4,4096]{1,0:T(4,128)S(1)} collective-permute-done((f32[4,4096]{1,0:T(4,128)S(1)}, f32[4,4096]{1,0:T(4,128)S(1)}, u32[]{:S(2)}, u32[]{:S(2)}) %collective-permute-start.7) | collective-permute-done | bytes 65568 | tf_op jit(solution)/shard_map/ppermute | solution.py:16
  295.7 4.9 %collective-permute-done.8 = f32[4,4096]{1,0:T(4,128)S(1)} collective-permute-done((f32[4,4096]{1,0:T(4,128)S(1)}, f32[4,4096]{1,0:T(4,128)S(1)}, u32[]{:S(2)}, u32[]{:S(2)}) %collective-permute-start.8) | collective-permute-done | bytes 65568 | tf_op jit(solution)/shard_map/ppermute | solution.py:16
  301.2 4.9 %collective-permute-done.9 = f32[4,4096]{1,0:T(4,128)S(1)} collective-permute-done((f32[4,4096]{1,0:T(4,128)S(1)}, f32[4,4096]{1,0:T(4,128)S(1)}, u32[]{:S(2)}, u32[]{:S(2)}) %collective-permute-start.9) | collective-permute-done | bytes 65568 | tf_op jit(solution)/shard_map/ppermute | solution.py:16
  306.7 4.9 %collective-permute-done.10 = f32[4,4096]{1,0:T(4,128)S(1)} collective-permute-done((f32[4,4096]{1,0:T(4,128)S(1)}, f32[4,4096]{1,0:T(4,128)S(1)}, u32[]{:S(2)}, u32[]{:S(2)}) %collective-permute-start.10) | collective-permute-done | bytes 65568 | tf_op jit(solution)/shard_map/ppermute | solution.py:16
  312.3 4.9 %collective-permute-done.11 = f32[4,4096]{1,0:T(4,128)S(1)} collective-permute-done((f32[4,4096]{1,0:T(4,128)S(1)}, f32[4,4096]{1,0:T(4,128)S(1)}, u32[]{:S(2)}, u32[]{:S(2)}) %collective-permute-start.11) | collective-permute-done | bytes 65568 | tf_op jit(solution)/shard_map/ppermute | solution.py:16
  317.8 4.9 %collective-permute-done.12 = f32[4,4096]{1,0:T(4,128)S(1)} collective-permute-done((f32[4,4096]{1,0:T(4,128)S(1)}, f32[4,4096]{1,0:T(4,128)S(1)}, u32[]{:S(2)}, u32[]{:S(2)}) %collective-permute-start.12) | collective-permute-done | bytes 65568 | tf_op jit(solution)/shard_map/ppermute | solution.py:16
  323.3 4.9 %collective-permute-done.13 = f32[4,4096]{1,0:T(4,128)S(1)} collective-permute-done((f32[4,4096]{1,0:T(4,128)S(1)}, f32[4,4096]{1,0:T(4,128)S(1)}, u32[]{:S(2)}, u32[]{:S(2)}) %collective-permute-start.13) | collective-permute-done | bytes 65568 | tf_op jit(solution)/shard_map/ppermute | solution.py:16
  328.8 4.4 %collective-permute-done.14 = f32[4,4096]{1,0:T(4,128)} collective-permute-done((f32[4,4096]{1,0:T(4,128)S(1)}, f32[4,4096]{1,0:T(4,128)}, u32[]{:S(2)}, u32[]{:S(2)}) %collective-permute-start.14) | collective-permute-done | bytes 65568 | tf_op jit(solution)/shard_map/ppermute | solution.py:16
  333.3 11.2 %concatenate.6 = f32[128,4096]{1,0:T(8,128)S(1)} concatenate(f32[4,4096]{1,0:T(4,128)} %collective-permute-done.14, f32[4,4096]{1,0:T(4,128)} %copy-done.8, f32[4,4096]{1,0:T(4,128)} %copy-done.7, f32[4,4096]{1,0:T(4,128)} %copy-done.6, f32[4,4096]{1,0:T(4,128)} %copy-done.5, f32[4,4096]{1,0:T(4,128)} %copy-done.4, f32[4,4096]{1,0:T(4,128)} %copy-done.3, f32[4,4096]{1,0:T(4,128)} %copy-done.2, ...), dimensions={0} | concatenate | bytes 4194304 | tf_op jit(solution)/shard_map/jit(_roll_dynamic)/concatenate | solution.py:19
  348.5 5.8 %cholesky.17 = f32[64,64]{1,0:T(8,128)S(1)} custom-call(f32[64,64]{1,0:T(8,128)S(1)} %fusion.14), custom_call_target="Cholesky" | custom-call | tf_op jit(solution)/shard_map/jit(cholesky)/cholesky | solution.py:54
  355.7 4.9 %custom-call.8 = f32[1,64,64]{1,2,0:T(8,128)S(1)} custom-call(f32[1,64,64]{2,1,0:T(8,128)S(1)} %fusion.8), custom_call_target="InvertDiagBlocksLowerTriangular" | custom-call | tf_op jit(solution)/shard_map/triangular_solve | solution.py:56
  (60 shorter events, 22.0 us)
Async XLA Ops:
  6.5 43.8 %copy-start = (bf16[1,128,4096]{2,1,0:T(8,128)(2,1)S(1)}, bf16[1,128,4096]{2,1,0:T(8,128)(2,1)}, u32[]{:S(2)}) copy-start(bf16[1,128,4096]{2,1,0:T(8,128)(2,1)} %param.8) | copy-start | bytes 3145732
  6.5 89.0 %all-gather.3.cloned.1.call-start = ((), (), s32[]{:S(2)}) async-start(), calls=%async_computation.1 | async-start | bytes 2162688 | tf_op jit(solution)/shard_map/all_gather | solution.py:35
  7.3 247.2 %all-reduce.2.cloned.1.call-start = ((), (), s32[]{:S(2)}) async-start(), calls=%async_computation | async-start | bytes 131072 | tf_op jit(solution)/shard_map/psum | solution.py:48
  254.5 7.6 %collective-permute-start = (f32[4,4096]{1,0:T(4,128)}, f32[4,4096]{1,0:T(4,128)S(1)}, u32[]{:S(2)}, u32[]{:S(2)}) collective-permute-start(f32[4,4096]{1,0:T(4,128)} %all-reduce.2.cloned.1.call-done), channel_id=1, source_target_pairs={{0,32},{32,64},{64,96},{96,128},{128,160},{160,192},{192,224},{224... | collective-permute-start | bytes 196616 | tf_op jit(solution)/shard_map/ppermute | solution.py:16
  262.1 3.6 collective-permute-start.1
  265.6 4.3 %collective-permute-start.2 = (f32[4,4096]{1,0:T(4,128)S(1)}, f32[4,4096]{1,0:T(4,128)S(1)}, u32[]{:S(2)}, u32[]{:S(2)}) collective-permute-start(f32[4,4096]{1,0:T(4,128)S(1)} %collective-permute-done.1), channel_id=1, source_target_pairs={{0,32},{32,64},{64,96},{96,128},{128,160},{160,192},{192,224},{224... | collective-permute-start | bytes 196616 | tf_op jit(solution)/shard_map/ppermute | solution.py:16
  269.9 4.9 %collective-permute-start.3 = (f32[4,4096]{1,0:T(4,128)S(1)}, f32[4,4096]{1,0:T(4,128)S(1)}, u32[]{:S(2)}, u32[]{:S(2)}) collective-permute-start(f32[4,4096]{1,0:T(4,128)S(1)} %collective-permute-done.2), channel_id=1, source_target_pairs={{0,32},{32,64},{64,96},{96,128},{128,160},{160,192},{192,224},{224... | collective-permute-start | bytes 196616 | tf_op jit(solution)/shard_map/ppermute | solution.py:16
  274.8 4.9 %collective-permute-start.4 = (f32[4,4096]{1,0:T(4,128)S(1)}, f32[4,4096]{1,0:T(4,128)S(1)}, u32[]{:S(2)}, u32[]{:S(2)}) collective-permute-start(f32[4,4096]{1,0:T(4,128)S(1)} %collective-permute-done.3), channel_id=1, source_target_pairs={{0,32},{32,64},{64,96},{96,128},{128,160},{160,192},{192,224},{224... | collective-permute-start | bytes 196616 | tf_op jit(solution)/shard_map/ppermute | solution.py:16
  279.7 4.9 %collective-permute-start.5 = (f32[4,4096]{1,0:T(4,128)S(1)}, f32[4,4096]{1,0:T(4,128)S(1)}, u32[]{:S(2)}, u32[]{:S(2)}) collective-permute-start(f32[4,4096]{1,0:T(4,128)S(1)} %collective-permute-done.4), channel_id=1, source_target_pairs={{0,32},{32,64},{64,96},{96,128},{128,160},{160,192},{192,224},{224... | collective-permute-start | bytes 196616 | tf_op jit(solution)/shard_map/ppermute | solution.py:16
  284.6 4.9 %collective-permute-start.6 = (f32[4,4096]{1,0:T(4,128)S(1)}, f32[4,4096]{1,0:T(4,128)S(1)}, u32[]{:S(2)}, u32[]{:S(2)}) collective-permute-start(f32[4,4096]{1,0:T(4,128)S(1)} %collective-permute-done.5), channel_id=1, source_target_pairs={{0,32},{32,64},{64,96},{96,128},{128,160},{160,192},{192,224},{224... | collective-permute-start | bytes 196616 | tf_op jit(solution)/shard_map/ppermute | solution.py:16
  289.5 0.6 copy-start.1
  290.2 4.9 %collective-permute-start.7 = (f32[4,4096]{1,0:T(4,128)S(1)}, f32[4,4096]{1,0:T(4,128)S(1)}, u32[]{:S(2)}, u32[]{:S(2)}) collective-permute-start(f32[4,4096]{1,0:T(4,128)S(1)} %collective-permute-done.6), channel_id=1, source_target_pairs={{0,32},{32,64},{64,96},{96,128},{128,160},{160,192},{192,224},{224... | collective-permute-start | bytes 196616 | tf_op jit(solution)/shard_map/ppermute | solution.py:16
  295.7 4.9 %collective-permute-start.8 = (f32[4,4096]{1,0:T(4,128)S(1)}, f32[4,4096]{1,0:T(4,128)S(1)}, u32[]{:S(2)}, u32[]{:S(2)}) collective-permute-start(f32[4,4096]{1,0:T(4,128)S(1)} %collective-permute-done.7), channel_id=1, source_target_pairs={{0,32},{32,64},{64,96},{96,128},{128,160},{160,192},{192,224},{224... | collective-permute-start | bytes 196616 | tf_op jit(solution)/shard_map/ppermute | solution.py:16
  301.2 4.9 %collective-permute-start.9 = (f32[4,4096]{1,0:T(4,128)S(1)}, f32[4,4096]{1,0:T(4,128)S(1)}, u32[]{:S(2)}, u32[]{:S(2)}) collective-permute-start(f32[4,4096]{1,0:T(4,128)S(1)} %collective-permute-done.8), channel_id=1, source_target_pairs={{0,32},{32,64},{64,96},{96,128},{128,160},{160,192},{192,224},{224... | collective-permute-start | bytes 196616 | tf_op jit(solution)/shard_map/ppermute | solution.py:16
  306.1 0.6 copy-start.4
  306.7 4.9 %collective-permute-start.10 = (f32[4,4096]{1,0:T(4,128)S(1)}, f32[4,4096]{1,0:T(4,128)S(1)}, u32[]{:S(2)}, u32[]{:S(2)}) collective-permute-start(f32[4,4096]{1,0:T(4,128)S(1)} %collective-permute-done.9), channel_id=1, source_target_pairs={{0,32},{32,64},{64,96},{96,128},{128,160},{160,192},{192,224},{224... | collective-permute-start | bytes 196616 | tf_op jit(solution)/shard_map/ppermute | solution.py:16
  312.3 4.9 %collective-permute-start.11 = (f32[4,4096]{1,0:T(4,128)S(1)}, f32[4,4096]{1,0:T(4,128)S(1)}, u32[]{:S(2)}, u32[]{:S(2)}) collective-permute-start(f32[4,4096]{1,0:T(4,128)S(1)} %collective-permute-done.10), channel_id=1, source_target_pairs={{0,32},{32,64},{64,96},{96,128},{128,160},{160,192},{192,224},{224... | collective-permute-start | bytes 196616 | tf_op jit(solution)/shard_map/ppermute | solution.py:16
  317.2 0.6 copy-start.6
  317.8 4.9 %collective-permute-start.12 = (f32[4,4096]{1,0:T(4,128)S(1)}, f32[4,4096]{1,0:T(4,128)S(1)}, u32[]{:S(2)}, u32[]{:S(2)}) collective-permute-start(f32[4,4096]{1,0:T(4,128)S(1)} %collective-permute-done.11), channel_id=1, source_target_pairs={{0,32},{32,64},{64,96},{96,128},{128,160},{160,192},{192,224},{224... | collective-permute-start | bytes 196616 | tf_op jit(solution)/shard_map/ppermute | solution.py:16
  322.7 0.6 copy-start.7
  323.3 4.9 %collective-permute-start.13 = (f32[4,4096]{1,0:T(4,128)S(1)}, f32[4,4096]{1,0:T(4,128)S(1)}, u32[]{:S(2)}, u32[]{:S(2)}) collective-permute-start(f32[4,4096]{1,0:T(4,128)S(1)} %collective-permute-done.12), channel_id=1, source_target_pairs={{0,32},{32,64},{64,96},{96,128},{128,160},{160,192},{192,224},{224... | collective-permute-start | bytes 196616 | tf_op jit(solution)/shard_map/ppermute | solution.py:16
  328.2 0.6 copy-start.8
  328.2 5.0 %collective-permute-start.14 = (f32[4,4096]{1,0:T(4,128)S(1)}, f32[4,4096]{1,0:T(4,128)}, u32[]{:S(2)}, u32[]{:S(2)}) collective-permute-start(f32[4,4096]{1,0:T(4,128)S(1)} %collective-permute-done.13), channel_id=1, source_target_pairs={{0,32},{32,64},{64,96},{96,128},{128,160},{160,192},{192,224},{224... | collective-permute-start | bytes 196616 | tf_op jit(solution)/shard_map/ppermute | solution.py:16
  344.4 16.5 %copy-start.9 = (s32[64]{0:T(128)S(1)}, s32[64]{0:T(128)}, u32[]{:S(2)}) copy-start(s32[64]{0:T(128)} %param.12) | copy-start | bytes 772
  (3 other events, 1.9 us)
Sparse Core Ops, SparseCore 0:
  10.5 84.9 all-gather.2
  106.9 147.5 all-reduce.1
